TPU v7x, 32 devices: a whole 2x2x4 slice. The times are simulated.
32 devices in a mesh: groups: 2 (over y), ctx: 4 (over z), head: 2 (over x), tp: 2 (over core).
Axes of the slice: x: 2, y: 2, z: 4, core: 2. Of those that a mesh axis runs over, the one named last changes fastest.
Arguments:
- queries: bfloat16 [32, 2048, 128], P(('head', 'tp'), ('groups', 'ctx')), parts along dimension 1, may hold values from -80 to 80
- stretch_keys: bfloat16 [8, 2048, 128], P(('head', 'tp'), ('groups', 'ctx')), parts along dimension 1, may hold values from -120 to 120
- stretch_values: bfloat16 [8, 2048, 128], P(('head', 'tp'), ('groups', 'ctx')), parts along dimension 1, may hold values from -6 to 6
- cache_keys: bfloat16 [8, 32768, 128], P(('head', 'tp'), ('groups', 'ctx')), parts along dimension 1, may hold values from -6 to 6
- cache_values: bfloat16 [8, 32768, 128], P(('head', 'tp'), ('groups', 'ctx')), parts along dimension 1, may hold values from -6 to 6
- block_picks: int32 [4, 8, 16], P('groups'), parts along dimension 0, may hold values from 0 to 31, as said below
- block_table: int32 [64], P('groups'), parts along dimension 0, may hold values from 0 to 31, as said below
Outputs:
- attended: bfloat16 [32, 2048, 128], P(('head', 'tp'), ('groups', 'ctx')), parts along dimension 1
There are 2 independent parts, one for each index of `groups`. A program takes and returns all parts, laid end to end along the dimension named above; each array names one. Nothing has to cross between parts.
Inputs may be any that keep to these rules, and one draw needn't show every extreme that they name: `block_picks`: for each query block and KV head the 16 picks are different logical blocks; exactly 4 of them have slots on each of 4 different indices of ctx, slot s lying on index s // 8. `block_table`: A permutation of the 32 physical slots.
All inputs are finite; a program needn't handle non-finite values.
Results may differ from a plain program's by a relative error of at most 0.0032.
Values may be sent and summed in bfloat16 or wider, within the bound.
No kernel may reach another device: no remote copies, remote signals or barrier semaphores. Data moves between devices by JAX's collectives and lax.ppermute only.
A program may use at most 64 MiB of HBM per device.

v0:
```python
import jax
import jax.numpy as jnp
import numpy as np
from jax import lax
from jax.sharding import PartitionSpec as P

BLOCK = 512
TOPK = 16


def shifted(value, axis, by):
    count = lax.axis_size(axis)
    pairs = [(i, i + by) for i in range(count) if 0 <= i + by < count]
    return lax.ppermute(value, axis, pairs)


def as_sent(value):

    def short(part):
        return part.astype(jnp.bfloat16) if part.dtype == jnp.float32 else part

    return jax.tree.map(short, value)


def partner(value, axis, bit):
    mask = 2**bit
    pairs = [(source, source ^ mask) for source in range(lax.axis_size(axis))]
    return lax.ppermute(value, axis, pairs)


def lookup(lookup_table, indices):
    entries = jnp.arange(lookup_table.shape[0], dtype=jnp.int32)
    return jnp.sum(jnp.where(indices[..., None] == entries, lookup_table, 0), axis=-1)


def owner_rank(owners):
    ordinal = jnp.arange(owners.shape[-1], dtype=jnp.int32)
    before = (owners[..., :, None] == owners[..., None, :]) & (ordinal[None, :] < ordinal[:, None])
    return jnp.sum(before, axis=-1)


def pick_rows(source, indices):
    return source[indices]


def take_blocks(blocks, indices):
    return jax.vmap(pick_rows)(blocks, indices)


def attend(query_rows, all_keys, all_values, allowed_mask):
    tile_relevance = jnp.einsum(
        "rd,kd->rk", query_rows, all_keys, preferred_element_type=jnp.float32
    )
    tile_relevance = tile_relevance * query_rows.shape[-1] ** (-0.5)
    tile_relevance = jnp.where(allowed_mask, tile_relevance, -jnp.inf)
    row_max = jnp.max(tile_relevance, axis=-1, keepdims=True)
    weights = jnp.exp(tile_relevance - row_max)
    weight_sum = jnp.sum(weights, axis=-1, keepdims=True)
    mixed = jnp.einsum(
        "rk,kd->rd", weights.astype(jnp.bfloat16), all_values, preferred_element_type=jnp.float32
    )
    return (mixed / weight_sum).astype(jnp.bfloat16)


def shards(
    queries, stretch_keys, stretch_values, cache_keys, cache_values, block_picks, block_table
):
    kv_dev, tok_dev, head_dim = stretch_keys.shape
    q_per_kv = queries.shape[0] // kv_dev
    blocks_dev = cache_keys.shape[1] // BLOCK
    ctx_size = lax.axis_size("ctx")
    ctx_index = lax.axis_index("ctx")
    per_peer = max(1, TOPK // ctx_size)
    parity = ctx_index % 2
    head_ids = lax.axis_index(("head", "tp")) * kv_dev + jnp.arange(kv_dev, dtype=jnp.int32)
    selector = head_ids[:, None] == jnp.arange(block_picks.shape[1], dtype=jnp.int32)[None, :]
    my_picks = jnp.sum(jnp.where(selector[None, :, :, None], block_picks[:, None, :, :], 0), axis=2)
    physical = lookup(block_table, my_picks)
    owners = physical // blocks_dev
    in_owner = physical % blocks_dev
    peer_rank = owner_rank(owners)
    targets = np.arange(ctx_size) * tok_dev // BLOCK
    target_owner = owners[targets]
    target_rank = peer_rank[targets]
    target_local = in_owner[targets]
    slot_ids = jnp.arange(per_peer, dtype=jnp.int32)
    matched = (target_owner[:, :, None, :] == ctx_index) & (
        target_rank[:, :, None, :] == slot_ids[None, None, :, None]
    )
    chosen = jnp.sum(jnp.where(matched, target_local[:, :, None, :], 0), axis=-1)
    usable = jnp.any(matched, axis=-1)
    chosen = jnp.transpose(chosen, (1, 0, 2)).reshape(kv_dev, ctx_size * per_peer)
    usable = jnp.transpose(usable, (1, 0, 2)).reshape(kv_dev, ctx_size * per_peer)
    my_block = ctx_index * tok_dev // BLOCK
    my_owner = lax.dynamic_index_in_dim(owners, my_block, 0, keepdims=False)
    my_rank = lax.dynamic_index_in_dim(peer_rank, my_block, 0, keepdims=False)
    my_slot = my_owner * per_peer + my_rank
    prev_keys, prev_values = shifted((stretch_keys, stretch_values), "ctx", 1)
    half_rows = BLOCK // 2
    key_halves = cache_keys.reshape(kv_dev, blocks_dev * 2, half_rows, head_dim)
    value_halves = cache_values.reshape(kv_dev, blocks_dev * 2, half_rows, head_dim)
    row_side = jnp.asarray(np.repeat(np.arange(ctx_size) % 2, per_peer), jnp.int32)
    half_index = chosen * 2 + row_side[None, :]
    sent_keys = jnp.where(usable[:, :, None, None], take_blocks(key_halves, half_index), 0).astype(
        jnp.bfloat16
    )
    sent_values = jnp.where(
        usable[:, :, None, None], take_blocks(value_halves, half_index), 0
    ).astype(jnp.bfloat16)
    got_keys, got_values = (
        lax.all_to_all(sent_keys, "ctx", split_axis=1, concat_axis=1, tiled=True),
        lax.all_to_all(sent_values, "ctx", split_axis=1, concat_axis=1, tiled=True),
    )
    mine_keys = take_blocks(got_keys, my_slot)
    mine_values = take_blocks(got_values, my_slot)
    other_keys, other_values = (
        partner(as_sent(mine_keys), "ctx", 0).astype(mine_keys.dtype),
        partner(as_sent(mine_values), "ctx", 0).astype(mine_values.dtype),
    )
    first_keys = jnp.where(parity == 0, mine_keys, other_keys)
    second_keys = jnp.where(parity == 0, other_keys, mine_keys)
    first_values = jnp.where(parity == 0, mine_values, other_values)
    second_values = jnp.where(parity == 0, other_values, mine_values)
    live_keys = jnp.concatenate([first_keys, second_keys], axis=2)
    live_values = jnp.concatenate([first_values, second_values], axis=2)
    span_cols = TOPK * BLOCK
    live_keys = live_keys.reshape(kv_dev, span_cols, head_dim)
    live_values = live_values.reshape(kv_dev, span_cols, head_dim)
    all_keys = jnp.concatenate([live_keys, prev_keys, stretch_keys], axis=1)
    all_values = jnp.concatenate([live_values, prev_values, stretch_values], axis=1)
    query_rows = queries.reshape(kv_dev, q_per_kv * tok_dev, head_dim)
    step_rows = min(512, q_per_kv * tok_dev)
    columns = jnp.arange(span_cols + 2 * tok_dev, dtype=jnp.int32)

    def one_head(packed):
        q_head, k_head, v_head = packed
        q_steps = q_head.reshape(-1, step_rows, head_dim)
        starts = jnp.arange(q_steps.shape[0], dtype=jnp.int32) * step_rows

        def one_step(packed_block_step):
            q_block, first_row = packed_block_step
            position = (first_row + jnp.arange(step_rows, dtype=jnp.int32)) % tok_dev
            cache_part = columns[None, :] < span_cols
            earlier_part = (
                (columns[None, :] >= span_cols)
                & (columns[None, :] < span_cols + tok_dev)
                & (columns[None, :] - span_cols > position[:, None])
                & (ctx_index > 0)
            )
            own_part = (columns[None, :] >= span_cols + tok_dev) & (
                columns[None, :] - span_cols - tok_dev <= position[:, None]
            )
            return attend(q_block, k_head, v_head, cache_part | earlier_part | own_part)

        return lax.map(one_step, (q_steps, starts)).reshape(q_per_kv * tok_dev, head_dim)

    result = lax.map(one_head, (query_rows, all_keys, all_values))
    return result.reshape(kv_dev * q_per_kv, tok_dev, head_dim)


def solution(mesh):
    placed = (
        P(("head", "tp"), ("groups", "ctx"), None),
        P(("head", "tp"), ("groups", "ctx"), None),
        P(("head", "tp"), ("groups", "ctx"), None),
        P(("head", "tp"), ("groups", "ctx"), None),
        P(("head", "tp"), ("groups", "ctx"), None),
        P("groups", None, None),
        P("groups"),
    )
    return jax.shard_map(
        shards,
        mesh=mesh,
        in_specs=placed,
        out_specs=P(("head", "tp"), ("groups", "ctx"), None),
        check_vma=False,
    )
```

profile of v0, /device:TPU:0, one launch (start us, length us, event | category | flops | bytes accessed | tf_op | source)
XLA Modules:
  0.0 363.8 jit_solution(13856905821156815247)
XLA Ops:
  0.1 0.9 select_reduce_fusion.2
  1.0 0.9 select_reduce_fusion
  1.9 0.7 pad_clamp_fusion
  5.1 0.7 fusion.27
  5.8 2.1 gather_fusion.3
  7.9 3.9 %gather_fusion.5 = bf16[32,256,128]{2,1,0:T(8,128)(2,1)} fusion(bf16[2,16,256,128]{3,2,1,0:T(8,128)(2,1)} %bitcast.67, s32[32]{0:T(128)S(1)} %reshape.259), kind=kCustom, calls=%fused_computation.5 | custom fusion | bytes 4194560 | tf_op jit(solution)/shard_map/vmap()/gather | solution.py:43
  11.9 3.2 broadcast_select_fusion
  15.2 1.6 copy.18
  16.7 6.4 %all-to-all-start = ((bf16[2,16,256,128]{3,2,0,1:T(8,128)(2,1)}), bf16[2,16,256,128]{3,2,0,1:T(8,128)(2,1)S(1)}, u32[]{:S(2)}, u32[]{:S(2)}) async-start(bf16[2,16,256,128]{3,2,0,1:T(8,128)(2,1)} %copy.18), calls=%async_computation | async-start | bytes 4194304 | tf_op jit(solution)/shard_map/all_to_all | solution.py:111
  23.1 3.1 copy.19
  26.2 45.1 %all-to-all-done = bf16[2,16,256,128]{3,2,0,1:T(8,128)(2,1)S(1)} async-done(((bf16[2,16,256,128]{3,2,0,1:T(8,128)(2,1)}), bf16[2,16,256,128]{3,2,0,1:T(8,128)(2,1)S(1)}, u32[]{:S(2)}, u32[]{:S(2)}) %all-to-all-start) | async-done | bytes 2097184 | tf_op jit(solution)/shard_map/all_to_all | solution.py:111
  71.3 4.5 %all-to-all-start.1 = ((bf16[2,16,256,128]{3,2,0,1:T(8,128)(2,1)}), bf16[2,16,256,128]{3,2,0,1:T(8,128)(2,1)}, u32[]{:S(2)}, u32[]{:S(2)}) async-start(bf16[2,16,256,128]{3,2,0,1:T(8,128)(2,1)} %copy.19), calls=%async_computation.1 | async-start | bytes 4194304 | tf_op jit(solution)/shard_map/all_to_all | solution.py:112
  75.9 2.6 gather_fusion.4
  78.5 2.0 collective-permute-start
  80.5 43.2 %all-to-all-done.1 = bf16[2,16,256,128]{3,2,0,1:T(8,128)(2,1)} async-done(((bf16[2,16,256,128]{3,2,0,1:T(8,128)(2,1)}), bf16[2,16,256,128]{3,2,0,1:T(8,128)(2,1)}, u32[]{:S(2)}, u32[]{:S(2)}) %all-to-all-start.1) | async-done | bytes 2097184 | tf_op jit(solution)/shard_map/all_to_all | solution.py:112
  123.7 3.7 %gather_fusion.6 = bf16[32,256,128]{2,1,0:T(8,128)(2,1)} fusion(bf16[2,16,256,128]{3,2,0,1:T(8,128)(2,1)} %all-to-all-done.1, s32[32]{0:T(128)S(1)} %reshape.265), kind=kCustom, calls=%fused_computation.6 | custom fusion | bytes 4194560 | tf_op jit(solution)/shard_map/vmap()/gather | solution.py:43
  127.4 3.9 %collective-permute-start.3 = (bf16[2,256,128]{2,1,0:T(8,128)(2,1)S(1)}, bf16[2,256,128]{2,1,0:T(8,128)(2,1)S(1)}, u32[]{:S(2)}, u32[]{:S(2)}) collective-permute-start(bf16[2,256,128]{2,1,0:T(8,128)(2,1)S(1)} %copy-done.5), channel_id=1, source_target_pairs={{0,4},{4,8},{8,12},{1,5},{5,9},{9,13},{2,6},{6,10},{10,14},{3,7},{... | collective-permute-start | bytes 393224 | tf_op jit(solution)/shard_map/ppermute | solution.py:14
  131.4 2.6 collective-permute-start.1
  134.0 24.2 %collective-permute-done = bf16[2,16,256,128]{3,2,1,0:T(8,128)(2,1)} collective-permute-done((bf16[2,16,256,128]{3,2,1,0:T(8,128)(2,1)S(1)}, bf16[2,16,256,128]{3,2,1,0:T(8,128)(2,1)}, u32[]{:S(2)}, u32[]{:S(2)}) %collective-permute-start) | collective-permute-done | bytes 2097184 | tf_op jit(solution)/shard_map/ppermute | solution.py:28
  158.2 43.1 %collective-permute-done.2 = bf16[2,16,256,128]{3,2,1,0:T(8,128)(2,1)} collective-permute-done((bf16[2,16,256,128]{3,2,1,0:T(8,128)(2,1)}, bf16[2,16,256,128]{3,2,1,0:T(8,128)(2,1)}, u32[]{:S(2)}, u32[]{:S(2)}) %collective-permute-start.2) | collective-permute-done | bytes 2097184 | tf_op jit(solution)/shard_map/ppermute | solution.py:28
  201.3 3.1 broadcast_select_fusion.3
  204.9 10.0 %pad_maximum_fusion.1 = bf16[2,8704,128]{2,1,0:T(8,128)(2,1)} fusion(bf16[2,256,128]{2,1,0:T(8,128)(2,1)S(1)} %copy-done.5, bf16[2,256,128]{2,1,0:T(8,128)(2,1)S(1)} %collective-permute-done.3, bf16[2,8192,128]{2,1,0:T(8,128)(2,1)S(1)} %bitcast.56), kind=kLoop, calls=%fused_computation.36 | loop fusion | flops 13369344 | bytes 8912896 | tf_op jit(solution)/shard_map/concatenate | solution.py:130
  215.3 9.9 %pad_maximum_fusion = bf16[2,8704,128]{2,1,0:T(8,128)(2,1)} fusion(bf16[2,256,128]{2,1,0:T(8,128)(2,1)S(1)} %copy-done.6, bf16[2,256,128]{2,1,0:T(8,128)(2,1)S(1)} %collective-permute-done.1, bf16[2,8192,128]{2,1,0:T(8,128)(2,1)S(1)} %bitcast.57), kind=kLoop, calls=%fused_computation.35 | loop fusion | flops 13369344 | bytes 8912896 | tf_op jit(solution)/shard_map/concatenate | solution.py:129
  225.2 136.7 %while.49 = (s32[]{:T(128)}, bf16[2,1024,128]{2,1,0:T(8,128)(2,1)S(1)}, bf16[2,1024,128]{2,1,0:T(8,128)(2,1)S(1)}, bf16[2,8704,128]{2,1,0:T(8,128)(2,1)}, bf16[2...) while((s32[]{:T(128)}, ...), condition=%wide.region_10.11_spmd.clone.clone, body=%wide.region_5.10_spmd.clone.clone.sunk | while | flops 2344288768 | bytes 68473648 | solution.py:157
  225.2 3.9 %dynamic-slice_bitcast_fusion.3 = (bf16[8704,128]{1,0:T(8,128)(2,1)}, bf16[8704,128]{1,0:T(8,128)(2,1)}) fusion(bf16[2,8704,128]{2,1,0:T(8,128)(2,1)} %get-tuple-element.681, s32[]{:T(128)} %get-tuple-element.668, bf16[2,8704,128]{2,1,0:T(8,128)(2,1)} %get-tuple-element.680), kind=kLoop, calls=%fused_computation.30.clone.1 | loop fusion | bytes 8912900 | tf_op jit(solution)/shard_map/while/body/jit(dynamic_index_in_dim)/squeeze | solution.py:157
  229.2 64.4 %while.50 = (s32[]{:T(128)}, bf16[2,512,128]{2,1,0:T(8,128)(2,1)S(1)}, s32[8704]{0:T(1024)S(1)}, s32[2]{0:T(128)S(1)}, pred[]{:T(512)}, /*index=5*/bf16[2,512,12...) while((s32[]{:T(128)}, ...), condition=%wide.region_9.9_spmd.clone, body=%wide.region_6.8_spmd.clone.sunk | while | flops 2344288768 | bytes 58477172 | solution.py:155
  229.2 0.6 dynamic_slice.85
  229.8 0.6 add_select_fusion.2
  230.4 13.1 %fusion.43 = (f32[512]{0:T(512)S(1)}, f32[512,8704]{1,0:T(8,128)}) fusion(bf16[8704,128]{1,0:T(8,128)(2,1)} %get-tuple-element.656, bf16[2,512,128]{2,1,0:T(8,128)(2,1)S(1)} %get-tuple-element.655, s32[]{:T(128)} %get-tuple-element.641, s32[8704]{0:T(1024)S(1)} %get-tuple-element.625, pred[8704]{0:T(1024)(128)(4,1)S(1)} %get-tuple-element.626, ...), kind=kOutput, calls=%fused_computation.75.clone.1 | convolution fusion | flops 1185414656 | bytes 20290564 | tf_op jit(solution)/shard_map/while/body/eval_jaxpr/while/body/eval_jaxpr/rd,kd->rk/dot_general | solution.py:51
  243.5 8.5 %fusion.44 = f32[512]{0:T(512)S(1)} fusion(f32[512,8704]{1,0:T(8,128)} %get-tuple-element.630, f32[512]{0:T(512)S(1)} %get-tuple-element.631), kind=kLoop, calls=%fused_computation.10.clone.1 | loop fusion | flops 8912384 | bytes 17829888 | tf_op jit(solution)/shard_map/while/body/eval_jaxpr/while/body/eval_jaxpr/reduce_sum | solution.py:58
  252.1 9.3 %fusion.45 = bf16[2,512,128]{2,1,0:T(8,128)(2,1)S(1)} fusion(bf16[2,512,128]{2,1,0:T(8,128)(2,1)S(1)} %get-tuple-element.642, s32[]{:T(128)} %get-tuple-element.641, bf16[8704,128]{1,0:T(8,128)(2,1)} %get-tuple-element.657, f32[512,8704]{1,0:T(8,128)} %get-tuple-element.630, f32[512]{0:T(512)S(1)} %get-tuple-element.631, f32[512]{0:T(512)S(1)} %fusion.44), kind=kOutput, calls=%fused_computation.17.clone.1 | convolution fusion | flops 1149894656 | bytes 20189188 | tf_op jit(solution)/shard_map/while/body/eval_jaxpr/while/body/eval_jaxpr/rk,kd->rd/dot_general | solution.py:59
  261.4 0.6 dynamic_slice.85
  262.0 0.6 add_select_fusion.2
  262.6 13.1 %fusion.43 = (f32[512]{0:T(512)S(1)}, f32[512,8704]{1,0:T(8,128)}) fusion(bf16[8704,128]{1,0:T(8,128)(2,1)} %get-tuple-element.656, bf16[2,512,128]{2,1,0:T(8,128)(2,1)S(1)} %get-tuple-element.655, s32[]{:T(128)} %get-tuple-element.641, s32[8704]{0:T(1024)S(1)} %get-tuple-element.625, pred[8704]{0:T(1024)(128)(4,1)S(1)} %get-tuple-element.626, ...), kind=kOutput, calls=%fused_computation.75.clone.1 | convolution fusion | flops 1185414656 | bytes 20290564 | tf_op jit(solution)/shard_map/while/body/eval_jaxpr/while/body/eval_jaxpr/rd,kd->rk/dot_general | solution.py:51
  275.7 8.5 %fusion.44 = f32[512]{0:T(512)S(1)} fusion(f32[512,8704]{1,0:T(8,128)} %get-tuple-element.630, f32[512]{0:T(512)S(1)} %get-tuple-element.631), kind=kLoop, calls=%fused_computation.10.clone.1 | loop fusion | flops 8912384 | bytes 17829888 | tf_op jit(solution)/shard_map/while/body/eval_jaxpr/while/body/eval_jaxpr/reduce_sum | solution.py:58
  284.2 9.3 %fusion.45 = bf16[2,512,128]{2,1,0:T(8,128)(2,1)S(1)} fusion(bf16[2,512,128]{2,1,0:T(8,128)(2,1)S(1)} %get-tuple-element.642, s32[]{:T(128)} %get-tuple-element.641, bf16[8704,128]{1,0:T(8,128)(2,1)} %get-tuple-element.657, f32[512,8704]{1,0:T(8,128)} %get-tuple-element.630, f32[512]{0:T(512)S(1)} %get-tuple-element.631, f32[512]{0:T(512)S(1)} %fusion.44), kind=kOutput, calls=%fused_computation.17.clone.1 | convolution fusion | flops 1149894656 | bytes 20189188 | tf_op jit(solution)/shard_map/while/body/eval_jaxpr/while/body/eval_jaxpr/rk,kd->rd/dot_general | solution.py:59
  293.6 3.9 %dynamic-slice_bitcast_fusion.3 = (bf16[8704,128]{1,0:T(8,128)(2,1)}, bf16[8704,128]{1,0:T(8,128)(2,1)}) fusion(bf16[2,8704,128]{2,1,0:T(8,128)(2,1)} %get-tuple-element.681, s32[]{:T(128)} %get-tuple-element.668, bf16[2,8704,128]{2,1,0:T(8,128)(2,1)} %get-tuple-element.680), kind=kLoop, calls=%fused_computation.30.clone.1 | loop fusion | bytes 8912900 | tf_op jit(solution)/shard_map/while/body/jit(dynamic_index_in_dim)/squeeze | solution.py:157
  297.5 64.4 %while.50 = (s32[]{:T(128)}, bf16[2,512,128]{2,1,0:T(8,128)(2,1)S(1)}, s32[8704]{0:T(1024)S(1)}, s32[2]{0:T(128)S(1)}, pred[]{:T(512)}, /*index=5*/bf16[2,512,12...) while((s32[]{:T(128)}, ...), condition=%wide.region_9.9_spmd.clone, body=%wide.region_6.8_spmd.clone.sunk | while | flops 2344288768 | bytes 58477172 | solution.py:155
  298.2 0.6 add_select_fusion.2
  298.8 13.1 %fusion.43 = (f32[512]{0:T(512)S(1)}, f32[512,8704]{1,0:T(8,128)}) fusion(bf16[8704,128]{1,0:T(8,128)(2,1)} %get-tuple-element.656, bf16[2,512,128]{2,1,0:T(8,128)(2,1)S(1)} %get-tuple-element.655, s32[]{:T(128)} %get-tuple-element.641, s32[8704]{0:T(1024)S(1)} %get-tuple-element.625, pred[8704]{0:T(1024)(128)(4,1)S(1)} %get-tuple-element.626, ...), kind=kOutput, calls=%fused_computation.75.clone.1 | convolution fusion | flops 1185414656 | bytes 20290564 | tf_op jit(solution)/shard_map/while/body/eval_jaxpr/while/body/eval_jaxpr/rd,kd->rk/dot_general | solution.py:51
  311.9 8.5 %fusion.44 = f32[512]{0:T(512)S(1)} fusion(f32[512,8704]{1,0:T(8,128)} %get-tuple-element.630, f32[512]{0:T(512)S(1)} %get-tuple-element.631), kind=kLoop, calls=%fused_computation.10.clone.1 | loop fusion | flops 8912384 | bytes 17829888 | tf_op jit(solution)/shard_map/while/body/eval_jaxpr/while/body/eval_jaxpr/reduce_sum | solution.py:58
  320.4 9.3 %fusion.45 = bf16[2,512,128]{2,1,0:T(8,128)(2,1)S(1)} fusion(bf16[2,512,128]{2,1,0:T(8,128)(2,1)S(1)} %get-tuple-element.642, s32[]{:T(128)} %get-tuple-element.641, bf16[8704,128]{1,0:T(8,128)(2,1)} %get-tuple-element.657, f32[512,8704]{1,0:T(8,128)} %get-tuple-element.630, f32[512]{0:T(512)S(1)} %get-tuple-element.631, f32[512]{0:T(512)S(1)} %fusion.44), kind=kOutput, calls=%fused_computation.17.clone.1 | convolution fusion | flops 1149894656 | bytes 20189188 | tf_op jit(solution)/shard_map/while/body/eval_jaxpr/while/body/eval_jaxpr/rk,kd->rd/dot_general | solution.py:59
  330.4 0.6 add_select_fusion.2
  331.0 13.1 %fusion.43 = (f32[512]{0:T(512)S(1)}, f32[512,8704]{1,0:T(8,128)}) fusion(bf16[8704,128]{1,0:T(8,128)(2,1)} %get-tuple-element.656, bf16[2,512,128]{2,1,0:T(8,128)(2,1)S(1)} %get-tuple-element.655, s32[]{:T(128)} %get-tuple-element.641, s32[8704]{0:T(1024)S(1)} %get-tuple-element.625, pred[8704]{0:T(1024)(128)(4,1)S(1)} %get-tuple-element.626, ...), kind=kOutput, calls=%fused_computation.75.clone.1 | convolution fusion | flops 1185414656 | bytes 20290564 | tf_op jit(solution)/shard_map/while/body/eval_jaxpr/while/body/eval_jaxpr/rd,kd->rk/dot_general | solution.py:51
  344.1 8.5 %fusion.44 = f32[512]{0:T(512)S(1)} fusion(f32[512,8704]{1,0:T(8,128)} %get-tuple-element.630, f32[512]{0:T(512)S(1)} %get-tuple-element.631), kind=kLoop, calls=%fused_computation.10.clone.1 | loop fusion | flops 8912384 | bytes 17829888 | tf_op jit(solution)/shard_map/while/body/eval_jaxpr/while/body/eval_jaxpr/reduce_sum | solution.py:58
  352.6 9.3 %fusion.45 = bf16[2,512,128]{2,1,0:T(8,128)(2,1)S(1)} fusion(bf16[2,512,128]{2,1,0:T(8,128)(2,1)S(1)} %get-tuple-element.642, s32[]{:T(128)} %get-tuple-element.641, bf16[8704,128]{1,0:T(8,128)(2,1)} %get-tuple-element.657, f32[512,8704]{1,0:T(8,128)} %get-tuple-element.630, f32[512]{0:T(512)S(1)} %get-tuple-element.631, f32[512]{0:T(512)S(1)} %fusion.44), kind=kOutput, calls=%fused_computation.17.clone.1 | convolution fusion | flops 1149894656 | bytes 20189188 | tf_op jit(solution)/shard_map/while/body/eval_jaxpr/while/body/eval_jaxpr/rk,kd->rd/dot_general | solution.py:59
  362.0 0.8 copy-done.7
  362.8 1.0 copy-done.1
  (59 shorter events, 5.2 us)
Async XLA Ops:
  0.0 5.8 %copy-start = (bf16[2,4096,128]{2,1,0:T(8,128)(2,1)S(1)}, bf16[2,4096,128]{2,1,0:T(8,128)(2,1)}, u32[]{:S(2)}) copy-start(bf16[2,4096,128]{2,1,0:T(8,128)(2,1)} %param.19) | copy-start | bytes 6291460
  7.9 4.0 %copy-start.3 = (bf16[32,256,128]{2,1,0:T(8,128)(2,1)S(1)}, bf16[32,256,128]{2,1,0:T(8,128)(2,1)}, u32[]{:S(2)}) copy-start(bf16[32,256,128]{2,1,0:T(8,128)(2,1)} %gather_fusion.3) | copy-start | bytes 6291460
  16.7 54.6 %all-to-all-start = ((bf16[2,16,256,128]{3,2,0,1:T(8,128)(2,1)}), bf16[2,16,256,128]{3,2,0,1:T(8,128)(2,1)S(1)}, u32[]{:S(2)}, u32[]{:S(2)}) async-start(bf16[2,16,256,128]{3,2,0,1:T(8,128)(2,1)} %copy.18), calls=%async_computation | async-start | bytes 4194304 | tf_op jit(solution)/shard_map/all_to_all | solution.py:111
  71.3 4.5 %copy-start.2 = (bf16[2,16,256,128]{3,2,0,1:T(8,128)(2,1)}, bf16[2,16,256,128]{3,2,0,1:T(8,128)(2,1)S(1)}, u32[]{:S(2)}) copy-start(bf16[2,16,256,128]{3,2,0,1:T(8,128)(2,1)S(1)} %all-to-all-done) | copy-start | bytes 6291460
  71.3 52.4 %all-to-all-start.1 = ((bf16[2,16,256,128]{3,2,0,1:T(8,128)(2,1)}), bf16[2,16,256,128]{3,2,0,1:T(8,128)(2,1)}, u32[]{:S(2)}, u32[]{:S(2)}) async-start(bf16[2,16,256,128]{3,2,0,1:T(8,128)(2,1)} %copy.19), calls=%async_computation.1 | async-start | bytes 4194304 | tf_op jit(solution)/shard_map/all_to_all | solution.py:112
  75.9 51.5 %copy-start.5 = (bf16[2,256,128]{2,1,0:T(8,128)(2,1)S(1)}, bf16[2,256,128]{2,1,0:T(8,128)(2,1)}, u32[]{:S(2)}) copy-start(bf16[2,256,128]{2,1,0:T(8,128)(2,1)} %param.18) | copy-start | bytes 393220
  75.9 55.5 %copy-start.6 = (bf16[2,256,128]{2,1,0:T(8,128)(2,1)S(1)}, bf16[2,256,128]{2,1,0:T(8,128)(2,1)}, u32[]{:S(2)}) copy-start(bf16[2,256,128]{2,1,0:T(8,128)(2,1)} %param.17) | copy-start | bytes 393220
  78.5 79.7 %collective-permute-start = (bf16[2,16,256,128]{3,2,1,0:T(8,128)(2,1)S(1)}, bf16[2,16,256,128]{3,2,1,0:T(8,128)(2,1)}, u32[]{:S(2)}, u32[]{:S(2)}) collective-permute-start(bf16[2,16,256,128]{3,2,1,0:T(8,128)(2,1)S(1)} %bitcast.58), channel_id=1, source_target_pairs={{0,4},{4,0},{8,12},{12,8},{1,5},{5,1},{9,13},{13,9},{2,6},{6,2},{1... | collective-permute-start | bytes 6291464 | tf_op jit(solution)/shard_map/ppermute | solution.py:28
  127.4 73.9 %collective-permute-start.2 = (bf16[2,16,256,128]{3,2,1,0:T(8,128)(2,1)}, bf16[2,16,256,128]{3,2,1,0:T(8,128)(2,1)}, u32[]{:S(2)}, u32[]{:S(2)}) collective-permute-start(bf16[2,16,256,128]{3,2,1,0:T(8,128)(2,1)} %bitcast.60), channel_id=1, source_target_pairs={{0,4},{4,0},{8,12},{12,8},{1,5},{5,1},{9,13},{13,9},{2,6},{6,2},{1... | collective-permute-start | bytes 6291464 | tf_op jit(solution)/shard_map/ppermute | solution.py:28
  127.4 77.5 %collective-permute-start.3 = (bf16[2,256,128]{2,1,0:T(8,128)(2,1)S(1)}, bf16[2,256,128]{2,1,0:T(8,128)(2,1)S(1)}, u32[]{:S(2)}, u32[]{:S(2)}) collective-permute-start(bf16[2,256,128]{2,1,0:T(8,128)(2,1)S(1)} %copy-done.5), channel_id=1, source_target_pairs={{0,4},{4,8},{8,12},{1,5},{5,9},{9,13},{2,6},{6,10},{10,14},{3,7},{... | collective-permute-start | bytes 393224 | tf_op jit(solution)/shard_map/ppermute | solution.py:14
  131.4 83.9 %collective-permute-start.1 = (bf16[2,256,128]{2,1,0:T(8,128)(2,1)S(1)}, bf16[2,256,128]{2,1,0:T(8,128)(2,1)S(1)}, u32[]{:S(2)}, u32[]{:S(2)}) collective-permute-start(bf16[2,256,128]{2,1,0:T(8,128)(2,1)S(1)} %copy-done.6), channel_id=1, source_target_pairs={{0,4},{4,8},{8,12},{1,5},{5,9},{9,13},{2,6},{6,10},{10,14},{3,7},{... | collective-permute-start | bytes 393224 | tf_op jit(solution)/shard_map/ppermute | solution.py:14
  215.3 9.9 %copy-start.4 = (bf16[8,256,128]{2,1,0:T(8,128)(2,1)S(1)}, bf16[8,256,128]{2,1,0:T(8,128)(2,1)}, u32[]{:S(2)}) copy-start(bf16[8,256,128]{2,1,0:T(8,128)(2,1)} %param.16) | copy-start | bytes 1572868
  362.0 0.8 copy-start.7
  362.0 1.8 copy-start.1
where the time goes:
time: 365 us; the launch traced here: 364 us
  waiting for transfers between devices  156 us (43%)
  matrix products  89.4 us (24%)
  other arithmetic  67.8 us (19%)
  local copies, waits for them, and re-layouts  31.2 us (9%)
  starting transfers between devices  19.4 us (5%)
    ppermute x2, waiting for transfers between devices, partner(): return lax.ppermute(value, axis, pairs)  67.3 us
    dot_general x4, matrix products, attend(): jnp.einsum('rd,kd->rk', query_rows, all_keys, preferred_element_type=jnp....  52.3 us
    all_to_all x1, waiting for transfers between devices, shards(): lax.all_to_all(sent_keys, 'ctx', split_axis=1, concat_axis=1, tiled=True)  45.1 us
    all_to_all x1, waiting for transfers between devices, shards(): lax.all_to_all(sent_values, 'ctx', split_axis=1, concat_axis=1, tiled=True)  43.2 us
    dot_general x4, matrix products, attend(): jnp.einsum('rk,kd->rd', weights.astype(jnp.bfloat16), all_values, preferr...  37.1 us
    reduce_sum x4, other arithmetic, attend(): weight_sum = jnp.sum(weights, axis=-1, keepdims=True)  34.2 us
    gather x6, local copies, waits for them, and re-layouts, pick_rows(): return source[indices]  12.5 us
    concatenate x1, other arithmetic, shards(): jnp.concatenate([live_values, prev_values, stretch_values], axis=1)  9.97 us
  transfers between devices with their start and end apart: 6, of which 4 were waited for; matrix products, arithmetic and copies ran while one was open for 6% of the time, Pallas kernels for 0%

commit v1 on v0

--- a/solution.py
+++ b/solution.py
@@ -1,7 +1,11 @@
+import functools
+
 import jax
 import jax.numpy as jnp
 import numpy as np
 from jax import lax
+from jax.experimental import pallas as pl
+from jax.experimental.pallas import tpu as pltpu
 from jax.sharding import PartitionSpec as P
 
 BLOCK = 512
@@ -62,7 +66,7 @@
     return (mixed / weight_sum).astype(jnp.bfloat16)
 
 
-def shards(
+def moved_blocks(
     queries, stretch_keys, stretch_values, cache_keys, cache_values, block_picks, block_table
 ):
     kv_dev, tok_dev, head_dim = stretch_keys.shape
@@ -158,6 +162,246 @@
     return result.reshape(kv_dev * q_per_kv, tok_dev, head_dim)
 
 
+LOG2E = 1.4426950408889634
+MASKED = -1e30
+STATS = 8
+
+
+def rotated(value, axis, by):
+    count = lax.axis_size(axis)
+    return lax.ppermute(value, axis, [(i, (i + by) % count) for i in range(count)])
+
+
+def dot(left, right, left_dim, right_dim):
+    dims = (((left_dim,), (right_dim,)), ((), ()))
+    return lax.dot_general(left, right, dims, preferred_element_type=jnp.float32)
+
+
+def split_three(row):
+    high = row.astype(jnp.bfloat16).astype(jnp.float32)
+    rest = row - high
+    mid = rest.astype(jnp.bfloat16).astype(jnp.float32)
+    return high, mid, rest - mid
+
+
+def pack_stats(row_max, row_sum):
+    parts = split_three(row_max) + split_three(row_sum)
+    shape = (STATS, row_max.shape[-1])
+    place = lax.broadcasted_iota(jnp.int32, shape, 0)
+    packed = jnp.zeros(shape, jnp.float32)
+    for index, part in enumerate(parts):
+        packed = jnp.where(place == index, jnp.broadcast_to(part, shape), packed)
+    return packed
+
+
+def unpack_stats(packed):
+    row_max = packed[0:1] + packed[1:2] + packed[2:3]
+    row_sum = packed[3:4] + packed[4:5] + packed[5:6]
+    return row_max, row_sum
+
+
+def soft_parts(score_tiles, value_tiles, unit):
+    row_max = functools.reduce(
+        jnp.maximum, [jnp.max(tile, axis=0, keepdims=True) for tile in score_tiles]
+    )
+    row_sum, mixed = 0.0, 0.0
+    for scores, values in zip(score_tiles, value_tiles):
+        weights = jnp.exp2((scores - row_max) * unit)
+        row_sum = row_sum + jnp.sum(weights, axis=0, keepdims=True)
+        mixed = mixed + dot(values(), weights.astype(jnp.bfloat16), 0, 0)
+    return row_max, row_sum, mixed
+
+
+def picked(slots_ref, first, count, cache_ref):
+    def load(index):
+        start = pl.multiple_of(slots_ref[first + index] * BLOCK, BLOCK)
+        return cache_ref[0, pl.ds(start, BLOCK), :]
+
+    return [functools.partial(load, index) for index in range(count)]
+
+
+def first_slot(hop, count, tok_dev, kv_dev, per_peer):
+    source = lax.rem(lax.axis_index("ctx") + count - hop, count)
+    return (source * tok_dev // BLOCK * kv_dev + pl.program_id(0)) * per_peer
+
+
+def part_kernel(hop, count, tok_dev, kv_dev, per_peer, step, unit, joined, *refs):
+    if joined:
+        slots_ref, q_ref, k_ref, v_ref, in_ref, out_ref = refs
+    else:
+        slots_ref, q_ref, k_ref, v_ref, out_ref = refs
+    head_dim = q_ref.shape[-1]
+    first = first_slot(hop, count, tok_dev, kv_dev, per_peer)
+    keys = picked(slots_ref, first, per_peer, k_ref)
+    values = picked(slots_ref, first, per_peer, v_ref)
+    for row in range(0, q_ref.shape[0], step):
+        rows = slice(row, row + step)
+        queries = q_ref[rows, :]
+        scores = [dot(load(), queries, 1, 1) for load in keys]
+        row_max, row_sum, mixed = soft_parts(scores, values, unit)
+        if joined:
+            there = in_ref[0, head_dim:, rows].astype(jnp.float32)
+            there_max, there_sum = unpack_stats(there)
+            top = jnp.maximum(row_max, there_max)
+            here_by = jnp.exp2((row_max - top) * unit)
+            there_sum = there_sum * jnp.exp2((there_max - top) * unit)
+            there_mixed = in_ref[0, :head_dim, rows].astype(jnp.float32)
+            row_max, row_sum = top, row_sum * here_by + there_sum
+            mixed = mixed * here_by + there_mixed * there_sum
+        out_ref[0, :head_dim, rows] = (mixed * (1.0 / row_sum)).astype(out_ref.dtype)
+        out_ref[0, head_dim:, rows] = pack_stats(row_max, row_sum).astype(out_ref.dtype)
+
+
+def own_kernel(
+    count, tok_dev, kv_dev, per_peer, step, unit, slots_ref, q_ref, k_ref, v_ref,
+    near_k_ref, near_v_ref, prev_ref, mixed_ref, stats_ref,
+):
+    head_dim = q_ref.shape[-1]
+    first = first_slot(0, count, tok_dev, kv_dev, per_peer)
+    keys = picked(slots_ref, first, per_peer, k_ref)
+    values = picked(slots_ref, first, per_peer, v_ref)
+    keys += [lambda: prev_ref[0, 0], lambda: near_k_ref[0]]
+    values += [lambda: prev_ref[1, 0], lambda: near_v_ref[0]]
+    shape = (tok_dev, step)
+    place = lax.broadcasted_iota(jnp.int32, shape, 0)
+    position = lax.broadcasted_iota(jnp.int32, shape, 1) % tok_dev
+    held = place <= position
+    before = (place > position) & (lax.axis_index("ctx") > 0)
+    for row in range(0, q_ref.shape[0], step):
+        rows = slice(row, row + step)
+        queries = q_ref[rows, :]
+        scores = [dot(load(), queries, 1, 1) for load in keys]
+        scores[-2] = jnp.where(before, scores[-2], MASKED)
+        scores[-1] = jnp.where(held, scores[-1], MASKED)
+        row_max, row_sum, mixed = soft_parts(scores, values, unit)
+        mixed_ref[0, :, rows] = mixed
+        where = lax.broadcasted_iota(jnp.int32, (STATS, step), 0)
+        stats_ref[0, :, rows] = jnp.where(where == 0, row_max, row_sum)
+
+
+def join_kernel(unit, mixed_ref, stats_ref, left_ref, right_ref, out_ref):
+    head_dim, step = mixed_ref.shape[1], out_ref.shape[1]
+    for index in range(out_ref.shape[0]):
+        rows = slice(index * step, (index + 1) * step)
+        stats = stats_ref[0, :, rows]
+        own_max, own_sum = stats[0:1], stats[1:2]
+        left_max, left_sum = unpack_stats(left_ref[0, head_dim:, rows].astype(jnp.float32))
+        right_max, right_sum = unpack_stats(right_ref[0, head_dim:, rows].astype(jnp.float32))
+        top = jnp.maximum(own_max, jnp.maximum(left_max, right_max))
+        own_by = jnp.exp2((own_max - top) * unit)
+        left_by = jnp.exp2((left_max - top) * unit) * left_sum
+        right_by = jnp.exp2((right_max - top) * unit) * right_sum
+        share = 1.0 / (own_sum * own_by + left_by + right_by)
+        mixed = mixed_ref[0, :, rows] * (own_by * share)
+        mixed += left_ref[0, :head_dim, rows].astype(jnp.float32) * (left_by * share)
+        mixed += right_ref[0, :head_dim, rows].astype(jnp.float32) * (right_by * share)
+        out_ref[index] = jnp.transpose(mixed).astype(out_ref.dtype)
+
+
+def moved_queries(
+    queries, stretch_keys, stretch_values, cache_keys, cache_values, block_picks, block_table
+):
+    kv_dev, tok_dev, head_dim = stretch_keys.shape
+    q_per_kv = queries.shape[0] // kv_dev
+    cache_rows = cache_keys.shape[1]
+    blocks_dev = cache_rows // BLOCK
+    count = lax.axis_size("ctx")
+    ctx_index = lax.axis_index("ctx")
+    per_peer = TOPK // count
+    rows = q_per_kv * tok_dev
+    step = min(512, rows)
+    unit = head_dim**-0.5 * LOG2E
+    flat = queries.reshape(kv_dev * rows, head_dim)
+    around = {0: flat}
+    for hop in range(1, count):
+        around[hop] = rotated(around[hop - 1], "ctx", 1)
+    prev = shifted(jnp.stack([stretch_keys, stretch_values]), "ctx", 1)
+
+    head_ids = lax.axis_index(("head", "tp")) * kv_dev + jnp.arange(kv_dev, dtype=jnp.int32)
+    selector = head_ids[:, None] == jnp.arange(block_picks.shape[1], dtype=jnp.int32)[None, :]
+    my_picks = jnp.sum(jnp.where(selector[None, :, :, None], block_picks[:, None, :, :], 0), axis=2)
+    physical = lookup(block_table, my_picks)
+    mine = physical // blocks_dev == ctx_index
+    rank = jnp.cumsum(mine.astype(jnp.int32), axis=-1) - 1
+    slot_ids = jnp.arange(per_peer, dtype=jnp.int32)
+    matched = mine[..., None, :] & (rank[..., None, :] == slot_ids[:, None])
+    slots = jnp.sum(jnp.where(matched, (physical % blocks_dev)[..., None, :], 0), axis=-1)
+    slots = slots.reshape(-1)
+
+    q_spec = pl.BlockSpec((rows, head_dim), lambda h, s: (h, 0))
+    cache_spec = pl.BlockSpec((1, cache_rows, head_dim), lambda h, s: (h, 0, 0))
+    near_spec = pl.BlockSpec((1, tok_dev, head_dim), lambda h, s: (h, 0, 0))
+    prev_spec = pl.BlockSpec((2, 1, tok_dev, head_dim), lambda h, s: (0, h, 0, 0))
+    part_spec = pl.BlockSpec((1, head_dim + STATS, rows), lambda h, s: (h, 0, 0))
+    part_shape = jax.ShapeDtypeStruct((kv_dev, head_dim + STATS, rows), jnp.bfloat16)
+    params = pltpu.CompilerParams(vmem_limit_bytes=48 << 20)
+
+    def cost(columns):
+        pairs = kv_dev * rows * columns
+        return pl.CostEstimate(
+            flops=8 * pairs * head_dim, bytes_accessed=8 << 20, transcendentals=pairs
+        )
+
+    def part(hop, given):
+        body = functools.partial(
+            part_kernel, hop, count, tok_dev, kv_dev, per_peer, step, unit, given is not None
+        )
+        extra = [] if given is None else [given]
+        return pl.pallas_call(
+            body,
+            out_shape=part_shape,
+            grid_spec=pltpu.PrefetchScalarGridSpec(
+                num_scalar_prefetch=1,
+                grid=(kv_dev,),
+                in_specs=[q_spec, cache_spec, cache_spec] + [part_spec] * len(extra),
+                out_specs=part_spec,
+            ),
+            compiler_params=params,
+            cost_estimate=cost(per_peer * BLOCK),
+            name=f"part{hop}",
+        )(slots, around[hop], cache_keys, cache_values, *extra)
+
+    left = rotated(part(1, None), "ctx", -1)
+    right = None
+    for hop in range(2, count):
+        right = rotated(part(hop, right), "ctx", 1)
+
+    mixed_shape = jax.ShapeDtypeStruct((kv_dev, head_dim, rows), jnp.float32)
+    stats_shape = jax.ShapeDtypeStruct((kv_dev, STATS, rows), jnp.float32)
+    mixed_spec = pl.BlockSpec((1, head_dim, rows), lambda h, *s: (h, 0, 0))
+    stats_spec = pl.BlockSpec((1, STATS, rows), lambda h, *s: (h, 0, 0))
+    mixed, stats = pl.pallas_call(
+        functools.partial(own_kernel, count, tok_dev, kv_dev, per_peer, step, unit),
+        out_shape=(mixed_shape, stats_shape),
+        grid_spec=pltpu.PrefetchScalarGridSpec(
+            num_scalar_prefetch=1,
+            grid=(kv_dev,),
+            in_specs=[q_spec, cache_spec, cache_spec, near_spec, near_spec, prev_spec],
+            out_specs=(mixed_spec, stats_spec),
+        ),
+        compiler_params=params,
+        cost_estimate=cost(per_peer * BLOCK + 2 * tok_dev),
+        name="own",
+    )(slots, flat, cache_keys, cache_values, stretch_keys, stretch_values, prev)
+
+    joined_spec = pl.BlockSpec((1, head_dim + STATS, rows), lambda h: (h, 0, 0))
+    return pl.pallas_call(
+        functools.partial(join_kernel, unit),
+        out_shape=jax.ShapeDtypeStruct(queries.shape, queries.dtype),
+        grid=(kv_dev,),
+        in_specs=[mixed_spec, stats_spec, joined_spec, joined_spec],
+        out_specs=pl.BlockSpec((q_per_kv, tok_dev, head_dim), lambda h: (h, 0, 0)),
+        compiler_params=params,
+        name="join",
+    )(mixed, stats, left, right)
+
+
+def shards(count, *arrays):
+    if count > 2 and TOPK % count == 0 and count <= 8:
+        return moved_queries(*arrays)
+    return moved_blocks(*arrays)
+
+
 def solution(mesh):
     placed = (
         P(("head", "tp"), ("groups", "ctx"), None),
@@ -169,7 +413,7 @@
         P("groups"),
     )
     return jax.shard_map(
-        shards,
+        functools.partial(shards, mesh.shape["ctx"]),
         mesh=mesh,
         in_specs=placed,
         out_specs=P(("head", "tp"), ("groups", "ctx"), None),

time: 365 us -> 95.7 us (0.26)
  waiting for transfers between devices: 156 us -> 47.3 us
  matrix products: 89.4 us -> 0 us
  other arithmetic: 67.8 us -> 2.32 us
  Pallas kernels: 0 us -> 33.8 us
  local copies, waits for them, and re-layouts: 31.2 us -> 3.29 us
  starting transfers between devices: 19.4 us -> 8.55 us
    dot_general x8 -> x0, matrix products: 89.4 us -> none  [the longest x4 52.3 us: attend(): jnp.einsum('rd,kd->rk', query_rows, all_keys, preferred_element_type=jnp....]
    all_to_all x2 -> x0, waiting for transfers between devices: 88.2 us -> none  [the longest x1 45.1 us: shards(): lax.all_to_all(sent_keys, 'ctx', split_axis=1, concat_axis=1, tiled=True)]
    reduce_sum x7 -> x2, other arithmetic: 35.5 us -> 0.93 us  [the longest x1 0.78 us: moved_queries(): jnp.sum(jnp.where(selector[None, :, :, None], block_picks[:, None, :, :],...]
    pallas_call x0 -> x5, Pallas kernels: none -> 33.8 us  [the longest x3 22.1 us: part(): pl.pallas_call(body, out_shape=part_shape, grid_spec=pltpu.PrefetchScalar...]
    concatenate x4 -> x0, other arithmetic: 20.7 us -> none  [the longest x1 9.97 us: shards(): jnp.concatenate([live_values, prev_values, stretch_values], axis=1)]
    ppermute x2 -> x6, waiting for transfers between devices: 67.3 us -> 47.3 us  [rotated(): lax.ppermute(value, axis, [(i, (i + by) % count) for i in range(count)])]
    gather x9 -> x0, local copies, waits for them, and re-layouts: 14.2 us -> none  [the longest x6 12.5 us: pick_rows(): return source[indices]]
    all_to_all x2 -> x0, starting transfers between devices: 10.8 us -> none  [the longest x1 6.36 us: shards(): lax.all_to_all(sent_keys, 'ctx', split_axis=1, concat_axis=1, tiled=True)]
  transfers between devices with their start and end apart: 6 -> 7, of which waited for: 4 -> 4; matrix products, arithmetic and copies ran while one was open for 6% -> 3% of each run, Pallas kernels for 0% -> 26%
where the time goes in v1:
time: 95.7 us; the launch traced here: 95.4 us
  waiting for transfers between devices  47.3 us (49%)
  Pallas kernels  33.8 us (35%)
  starting transfers between devices  8.55 us (9%)
  local copies, waits for them, and re-layouts  3.29 us (3%)
  other arithmetic  2.32 us (2%)
    ppermute x6, waiting for transfers between devices, rotated(): lax.ppermute(value, axis, [(i, (i + by) % count) for i in range(count)])  47.3 us
    pallas_call x3, Pallas kernels, part(): pl.pallas_call(body, out_shape=part_shape, grid_spec=pltpu.PrefetchScalar...  22.1 us
    pallas_call x1, Pallas kernels, moved_queries(): pl.pallas_call(functools.partial(own_kernel, count, tok_dev, kv_dev, per_...  10.4 us
    ppermute x6, starting transfers between devices, rotated(): lax.ppermute(value, axis, [(i, (i + by) % count) for i in range(count)])  5.94 us
    unnamed x12, local copies, waits for them, and re-layouts  3.2 us
    ppermute x1, starting transfers between devices, shifted(): return lax.ppermute(value, axis, pairs)  2.61 us
  transfers between devices with their start and end apart: 7, of which 4 were waited for; matrix products, arithmetic and copies ran while one was open for 3% of the time, Pallas kernels for 26%

profile of v1, /device:TPU:0, one launch (start us, length us, event | category | flops | bytes accessed | tf_op | source)
XLA Modules:
  0.0 95.4 jit_solution(11914782586811748794)
XLA Ops:
  0.0 3.1 %collective-permute-start.1 = (bf16[2048,128]{1,0:T(8,128)(2,1)}, bf16[2048,128]{1,0:T(8,128)(2,1)S(1)}, u32[]{:S(2)}, u32[]{:S(2)}) collective-permute-start(bf16[2048,128]{1,0:T(8,128)(2,1)} %bitcast.5), channel_id=1, source_target_pairs={{0,4},{4,8},{8,12},{12,0},{1,5},{5,9},{9,13},{13,1},{2,6},{6,10},{... | collective-permute-start | bytes 1572872 | tf_op jit(solution)/shard_map/ppermute | solution.py:172
  3.1 0.1 iota_compare_fusion.2
  3.1 0.8 select_reduce_fusion.1
  3.9 0.9 select_reduce_fusion
  4.8 12.4 %collective-permute-done.1.refs_1_ = bf16[2048,128]{1,0:T(8,128)(2,1)S(1)} collective-permute-done((bf16[2048,128]{1,0:T(8,128)(2,1)}, bf16[2048,128]{1,0:T(8,128)(2,1)S(1)}, u32[]{:S(2)}, u32[]{:S(2)}) %collective-permute-start.1) | collective-permute-done | bytes 524320 | tf_op jit(solution)/shard_map/ppermute | solution.py:172
  17.2 0.0 collective-permute-start.3
  17.2 0.4 reduce_window_sum.11
  17.6 0.1 select_reduce_fusion.2
  17.8 0.1 reshape.90.slots_ref.refs_0_
  17.9 0.0 copy-start
  17.9 0.0 copy-start.1
  17.9 14.2 %collective-permute-done.3.refs_1_ = bf16[2048,128]{1,0:T(8,128)(2,1)S(1)} collective-permute-done((bf16[2048,128]{1,0:T(8,128)(2,1)S(1)}, bf16[2048,128]{1,0:T(8,128)(2,1)S(1)}, u32[]{:S(2)}, u32[]{:S(2)}) %collective-permute-start.3) | collective-permute-done | bytes 524320 | tf_op jit(solution)/shard_map/ppermute | solution.py:172
  32.1 0.0 copy-start.2
  32.1 1.6 %copy-done.2 = bf16[2,4096,128]{2,1,0:T(8,128)(2,1)S(1)} copy-done((bf16[2,4096,128]{2,1,0:T(8,128)(2,1)S(1)}, bf16[2,4096,128]{2,1,0:T(8,128)(2,1)}, u32[]{:S(2)}) %copy-start.2) | copy-done | bytes 2097176
  33.7 0.0 copy-start.4
  33.7 1.6 %copy-done.4 = bf16[2,4096,128]{2,1,0:T(8,128)(2,1)S(1)} copy-done((bf16[2,4096,128]{2,1,0:T(8,128)(2,1)S(1)}, bf16[2,4096,128]{2,1,0:T(8,128)(2,1)}, u32[]{:S(2)}) %copy-start.4) | copy-done | bytes 2097176
  35.3 7.3 %part2.1 = bf16[2,136,1024]{2,1,0:T(8,128)(2,1)S(1)} custom-call(s32[16]{0:T(128)S(1)} %reshape.90.slots_ref.refs_0_, bf16[2048,128]{1,0:T(8,128)(2,1)S(1)} %collective-permute-done.3.refs_1_, bf16[2,4096,128]{2,1,0:T(8,128)(2,1)S(1)} %copy-done.2, bf16[2,4096,128]{2,1,0:T(8,128)(2,1)S(1)} %copy-done.4), custom_call_target="tpu_custom_call" | custom-call | flops 4294967296 | bytes 8388608 | tf_op jit(solution)/shard_map/part2/pallas_call | solution.py:350
  42.6 0.1 collective-permute-start.5
  42.7 0.1 collective-permute-start.4
  42.8 0.0 copy-done
  42.8 0.0 copy-done.1
  42.8 2.6 %collective-permute-start = (bf16[2,2,256,128]{3,2,1,0:T(8,128)(2,1)S(1)}, bf16[2,2,256,128]{3,2,1,0:T(8,128)(2,1)S(1)}, u32[]{:S(2)}, u32[]{:S(2)}) collective-permute-start(bf16[2,2,256,128]{3,2,1,0:T(8,128)(2,1)S(1)} %pad_maximum_fusion), channel_id=1, source_target_pairs={{0,4},{4,8},{8,12},{1,5},{5,9},{9,13},{2,6},{6,10},{10,14},{3,7},{... | collective-permute-start | bytes 786440 | tf_op jit(solution)/shard_map/ppermute | solution.py:18
  45.4 7.3 %part1.1 = bf16[2,136,1024]{2,1,0:T(8,128)(2,1)S(1)} custom-call(s32[16]{0:T(128)S(1)} %reshape.90.slots_ref.refs_0_, bf16[2048,128]{1,0:T(8,128)(2,1)S(1)} %collective-permute-done.1.refs_1_, bf16[2,4096,128]{2,1,0:T(8,128)(2,1)S(1)} %copy-done.2, bf16[2,4096,128]{2,1,0:T(8,128)(2,1)S(1)} %copy-done.4), custom_call_target="tpu_custom_call" | custom-call | flops 4294967296 | bytes 8388608 | tf_op jit(solution)/shard_map/part1/pallas_call | solution.py:350
  52.8 0.0 copy-start.3
  52.8 0.0 copy-start.5
  52.8 2.5 %collective-permute-start.2 = (bf16[2,136,1024]{2,1,0:T(8,128)(2,1)S(1)}, bf16[2,136,1024]{2,1,0:T(8,128)(2,1)S(1)}, u32[]{:S(2)}, u32[]{:S(2)}) collective-permute-start(bf16[2,136,1024]{2,1,0:T(8,128)(2,1)S(1)} %part1.1), channel_id=1, source_target_pairs={{0,12},{4,0},{8,4},{12,8},{1,13},{5,1},{9,5},{13,9},{2,14},{6,2},{... | collective-permute-start | bytes 1671176 | tf_op jit(solution)/shard_map/ppermute | solution.py:172
  55.4 15.9 %collective-permute-done.4.refs_1_ = bf16[2048,128]{1,0:T(8,128)(2,1)S(1)} collective-permute-done((bf16[2048,128]{1,0:T(8,128)(2,1)S(1)}, bf16[2048,128]{1,0:T(8,128)(2,1)S(1)}, u32[]{:S(2)}, u32[]{:S(2)}) %collective-permute-start.4) | collective-permute-done | bytes 524320 | tf_op jit(solution)/shard_map/ppermute | solution.py:172
  71.3 0.0 collective-permute-done.5.refs_4_
  71.3 7.4 %part3.1 = bf16[2,136,1024]{2,1,0:T(8,128)(2,1)S(1)} custom-call(s32[16]{0:T(128)S(1)} %reshape.90.slots_ref.refs_0_, bf16[2048,128]{1,0:T(8,128)(2,1)S(1)} %collective-permute-done.4.refs_1_, bf16[2,4096,128]{2,1,0:T(8,128)(2,1)S(1)} %copy-done.2, bf16[2,4096,128]{2,1,0:T(8,128)(2,1)S(1)} %copy-done.4, bf16[2,136,1024]{2,1,0:T(8,128)(2,1)S(1)} %collective-permute-done.5.refs_4_), custom_call_target="tpu_custom_call" | custom-call | flops 4294967296 | bytes 8388608 | tf_op jit(solution)/shard_map/part3/pallas_call | solution.py:350
  78.7 0.2 collective-permute-start.6
  78.9 0.0 collective-permute-done.prev_ref
  79.0 0.0 copy-done.3
  79.0 0.0 copy-done.5
  79.0 10.4 %own.1 = (f32[2,128,1024]{2,1,0:T(8,128)S(1)}, f32[2,8,1024]{2,1,0:T(8,128)S(1)}) custom-call(s32[16]{0:T(128)S(1)} %reshape.90.slots_ref.refs_0_, bf16[2048,128]{1,0:T(8,128)(2,1)S(1)} %bitcast.6, bf16[2,4096,128]{2,1,0:T(8,128)(2,1)S(1)} %copy-done.3, bf16[2,4096,128]{2,1,0:T(8,128)(2,1)} %refs_3_.5, bf16[2,256,128]{2,1,0:T(8,128)(2,1)S(1)} %copy-done, ...), custom_call_target="tpu_custom_call" | custom-call | flops 5368709120 | bytes 8388608 | tf_op jit(solution)/shard_map/own/pallas_call | solution.py:373
  89.4 0.0 collective-permute-done.2.left_ref
  89.4 4.8 %collective-permute-done.6.right_ref = bf16[2,136,1024]{2,1,0:T(8,128)(2,1)S(1)} collective-permute-done((bf16[2,136,1024]{2,1,0:T(8,128)(2,1)S(1)}, bf16[2,136,1024]{2,1,0:T(8,128)(2,1)S(1)}, u32[]{:S(2)}, u32[]{:S(2)}) %collective-permute-start.6) | collective-permute-done | bytes 557088 | tf_op jit(solution)/shard_map/ppermute | solution.py:172
  94.2 1.2 %join.1 = bf16[8,256,128]{2,1,0:T(8,128)(2,1)} custom-call(f32[2,128,1024]{2,1,0:T(8,128)S(1)} %get-tuple-element.7.mixed_ref, f32[2,8,1024]{2,1,0:T(8,128)S(1)} %get-tuple-element.8.stats_ref, bf16[2,136,1024]{2,1,0:T(8,128)(2,1)S(1)} %collective-permute-done.2.left_ref, bf16[2,136,1024]{2,1,0:T(8,128)(2,1)S(1)} %collective-permute-done.6.right_ref), custom_call_target="tpu_custom_call" | custom-call | tf_op jit(solution)/shard_map/join/pallas_call | solution.py:388
  (4 shorter events, 0.1 us)
Async XLA Ops:
  0.0 17.2 %collective-permute-start.1 = (bf16[2048,128]{1,0:T(8,128)(2,1)}, bf16[2048,128]{1,0:T(8,128)(2,1)S(1)}, u32[]{:S(2)}, u32[]{:S(2)}) collective-permute-start(bf16[2048,128]{1,0:T(8,128)(2,1)} %bitcast.5), channel_id=1, source_target_pairs={{0,4},{4,8},{8,12},{12,0},{1,5},{5,9},{9,13},{13,1},{2,6},{6,10},{... | collective-permute-start | bytes 1572872 | tf_op jit(solution)/shard_map/ppermute | solution.py:172
  17.2 14.9 %collective-permute-start.3 = (bf16[2048,128]{1,0:T(8,128)(2,1)S(1)}, bf16[2048,128]{1,0:T(8,128)(2,1)S(1)}, u32[]{:S(2)}, u32[]{:S(2)}) collective-permute-start(bf16[2048,128]{1,0:T(8,128)(2,1)S(1)} %collective-permute-done.1.refs_1_), channel_id=1, source_target_pairs={{0,4},{4,8},{8,12},{12,0},{1,5},{5,9},{9,13},{13,1},{2,6},{6,10},{... | collective-permute-start | bytes 1572872 | tf_op jit(solution)/shard_map/ppermute | solution.py:172
  17.9 24.9 %copy-start = (bf16[2,256,128]{2,1,0:T(8,128)(2,1)S(1)}, bf16[2,256,128]{2,1,0:T(8,128)(2,1)}, u32[]{:S(2)}) copy-start(bf16[2,256,128]{2,1,0:T(8,128)(2,1)} %near_k_ref.1) | copy-start | bytes 393220
  17.9 24.9 %copy-start.1 = (bf16[2,256,128]{2,1,0:T(8,128)(2,1)S(1)}, bf16[2,256,128]{2,1,0:T(8,128)(2,1)}, u32[]{:S(2)}) copy-start(bf16[2,256,128]{2,1,0:T(8,128)(2,1)} %near_v_ref.1) | copy-start | bytes 393220
  32.1 1.6 %copy-start.2 = (bf16[2,4096,128]{2,1,0:T(8,128)(2,1)S(1)}, bf16[2,4096,128]{2,1,0:T(8,128)(2,1)}, u32[]{:S(2)}) copy-start(bf16[2,4096,128]{2,1,0:T(8,128)(2,1)} %refs_2_.5) | copy-start | bytes 6291460
  33.7 1.6 %copy-start.4 = (bf16[2,4096,128]{2,1,0:T(8,128)(2,1)S(1)}, bf16[2,4096,128]{2,1,0:T(8,128)(2,1)}, u32[]{:S(2)}) copy-start(bf16[2,4096,128]{2,1,0:T(8,128)(2,1)} %refs_3_.5) | copy-start | bytes 6291460
  42.6 28.6 %collective-permute-start.5 = (bf16[2,136,1024]{2,1,0:T(8,128)(2,1)S(1)}, bf16[2,136,1024]{2,1,0:T(8,128)(2,1)S(1)}, u32[]{:S(2)}, u32[]{:S(2)}) collective-permute-start(bf16[2,136,1024]{2,1,0:T(8,128)(2,1)S(1)} %part2.1), channel_id=1, source_target_pairs={{0,4},{4,8},{8,12},{12,0},{1,5},{5,9},{9,13},{13,1},{2,6},{6,10},{... | collective-permute-start | bytes 1671176 | tf_op jit(solution)/shard_map/ppermute | solution.py:172
  42.7 28.6 %collective-permute-start.4 = (bf16[2048,128]{1,0:T(8,128)(2,1)S(1)}, bf16[2048,128]{1,0:T(8,128)(2,1)S(1)}, u32[]{:S(2)}, u32[]{:S(2)}) collective-permute-start(bf16[2048,128]{1,0:T(8,128)(2,1)S(1)} %collective-permute-done.3.refs_1_), channel_id=1, source_target_pairs={{0,4},{4,8},{8,12},{12,0},{1,5},{5,9},{9,13},{13,1},{2,6},{6,10},{... | collective-permute-start | bytes 1572872 | tf_op jit(solution)/shard_map/ppermute | solution.py:172
  42.8 36.1 %collective-permute-start = (bf16[2,2,256,128]{3,2,1,0:T(8,128)(2,1)S(1)}, bf16[2,2,256,128]{3,2,1,0:T(8,128)(2,1)S(1)}, u32[]{:S(2)}, u32[]{:S(2)}) collective-permute-start(bf16[2,2,256,128]{3,2,1,0:T(8,128)(2,1)S(1)} %pad_maximum_fusion), channel_id=1, source_target_pairs={{0,4},{4,8},{8,12},{1,5},{5,9},{9,13},{2,6},{6,10},{10,14},{3,7},{... | collective-permute-start | bytes 786440 | tf_op jit(solution)/shard_map/ppermute | solution.py:18
  52.8 26.2 %copy-start.3 = (bf16[2,4096,128]{2,1,0:T(8,128)(2,1)S(1)}, bf16[2,4096,128]{2,1,0:T(8,128)(2,1)}, u32[]{:S(2)}) copy-start(bf16[2,4096,128]{2,1,0:T(8,128)(2,1)} %refs_2_.5) | copy-start | bytes 6291460
  52.8 26.2 %copy-start.5 = (bf16[8,256,128]{2,1,0:T(8,128)(2,1)S(1)}, bf16[8,256,128]{2,1,0:T(8,128)(2,1)}, u32[]{:S(2)}) copy-start(bf16[8,256,128]{2,1,0:T(8,128)(2,1)} %param.7) | copy-start | bytes 1572868
  52.8 36.6 %collective-permute-start.2 = (bf16[2,136,1024]{2,1,0:T(8,128)(2,1)S(1)}, bf16[2,136,1024]{2,1,0:T(8,128)(2,1)S(1)}, u32[]{:S(2)}, u32[]{:S(2)}) collective-permute-start(bf16[2,136,1024]{2,1,0:T(8,128)(2,1)S(1)} %part1.1), channel_id=1, source_target_pairs={{0,12},{4,0},{8,4},{12,8},{1,13},{5,1},{9,5},{13,9},{2,14},{6,2},{... | collective-permute-start | bytes 1671176 | tf_op jit(solution)/shard_map/ppermute | solution.py:172
  78.7 15.5 %collective-permute-start.6 = (bf16[2,136,1024]{2,1,0:T(8,128)(2,1)S(1)}, bf16[2,136,1024]{2,1,0:T(8,128)(2,1)S(1)}, u32[]{:S(2)}, u32[]{:S(2)}) collective-permute-start(bf16[2,136,1024]{2,1,0:T(8,128)(2,1)S(1)} %part3.1), channel_id=1, source_target_pairs={{0,4},{4,8},{8,12},{12,0},{1,5},{5,9},{9,13},{13,1},{2,6},{6,10},{... | collective-permute-start | bytes 1671176 | tf_op jit(solution)/shard_map/ppermute | solution.py:172
